TPU v7x, 32 devices: a whole 2x2x4 slice. The times are simulated.
32 devices in a mesh: freq: 4 (over y, core), space: 8 (over z, x).
Axes of the slice: x: 2, y: 2, z: 4, core: 2. Of those that a mesh axis runs over, the one named last changes fastest.
Arguments:
- traces: float32 [1024, 512, 256], P(('freq', 'space')), may hold values from -50 to 50
- probes: float32 [8, 128, 64], P('freq'), may hold values from -0.5 to 0.5
Outputs:
- denoised: float32 [1024, 512, 256], P(('freq', 'space'))
All inputs are finite; a program needn't handle non-finite values.
Results may differ from a plain program's by a relative error of at most 0.000092.
Values sent between devices are 32-bit elements; how exact they have to be, the bound alone decides.
No kernel may reach another device: no remote copies, remote signals or barrier semaphores. Data moves between devices by JAX's collectives and lax.ppermute only.
A program may use at most 192 MiB of HBM per device.

v0:
```python
import jax
import jax.numpy as jnp
from jax import lax
from jax.sharding import PartitionSpec as P

NT = 1024
BAND_LO = 16
HIGHEST_PRECISION = lax.Precision.HIGHEST


def wave_table(freq_ids, time_ids, period, factor):
    phase = (freq_ids[:, None] * time_ids[None, :] % period).astype(jnp.float32) * (
        2.0 * jnp.pi / period
    )
    return jnp.stack([jnp.cos(phase), -jnp.sin(phase)]) * factor


def hankel(spectrum, window, columns):
    width = spectrum.shape[-1]
    tiled = jnp.tile(spectrum, (1, 1, window + 1))[:, :, : window * (width + 1)]
    return tiled.reshape(spectrum.shape[0], spectrum.shape[1], window, width + 1)[:, :, :, :columns]


def diag_mean(blocks, width):
    halves, channels, window, columns = blocks.shape
    padded = jnp.pad(blocks, ((0, 0), (0, 0), (0, 0), (0, width + 1 - columns)))
    flat_rows = padded.reshape(halves, channels, window * (width + 1))
    flat_rows = jnp.pad(flat_rows, ((0, 0), (0, 0), (0, width - window)))
    totals = flat_rows.reshape(halves, channels, window + 1, width).sum(axis=2)
    position = jnp.arange(width, dtype=jnp.int32)
    counts = jnp.minimum(jnp.minimum(position + 1, width - position), min(window, columns))
    return totals / counts.astype(jnp.float32)


def assemble(gram_raw, cross_raw):
    half = gram_raw.shape[-1] // 2
    diagonal_part = gram_raw[..., :half, :half] + gram_raw[..., half:, half:]
    skew_part = gram_raw[..., half:, :half] - gram_raw[..., :half, half:]
    gram_matrix = jnp.concatenate(
        [
            jnp.concatenate([diagonal_part, skew_part], -1),
            jnp.concatenate([-skew_part, diagonal_part], -1),
        ],
        -2,
    )
    real_rows = cross_raw[..., 0, :, :]
    imag_rows = cross_raw[..., 1, :, :]
    cross_terms = jnp.concatenate(
        [
            real_rows[..., :half, :] + imag_rows[..., half:, :],
            imag_rows[..., :half, :] - real_rows[..., half:, :],
        ],
        -2,
    )
    return (gram_matrix, cross_terms)


def solve_one(factor_rows, right_rows):
    return jax.scipy.linalg.cho_solve((factor_rows, True), right_rows)


def first_pass(slice_pair):
    spectrum, probe = slice_pair
    width = spectrum.shape[-1]
    window = width // 2 + 1
    columns = width // 2
    channels = spectrum.shape[1]
    hankel_rows = hankel(spectrum, window, columns).reshape(2, channels * window, columns)
    sketch_basis = jnp.einsum(
        "qrp,pk->rqk", hankel_rows, probe, precision=HIGHEST_PRECISION
    ).reshape(channels * window, 2 * probe.shape[1])
    gram_raw = jnp.dot(sketch_basis.T, sketch_basis, precision=HIGHEST_PRECISION)
    cross_raw = jnp.einsum("rk,qrp->qkp", sketch_basis, hankel_rows, precision=HIGHEST_PRECISION)
    return (sketch_basis, gram_raw, cross_raw)


def body(traces, probes):
    time_slab = lax.all_to_all(traces, "space", split_axis=1, concat_axis=0, tiled=True)
    time_local = time_slab.shape[0]
    channels = time_slab.shape[1]
    width = time_slab.shape[2]
    freq_local = probes.shape[0]
    freq_total = freq_local * lax.axis_size("freq")
    time_ids = lax.axis_index("freq") * time_local + jnp.arange(time_local, dtype=jnp.int32)
    freq_ids = (
        BAND_LO + jnp.int32(0) + jnp.arange(lax.axis_size("freq") * freq_local, dtype=jnp.int32)
    )
    wave_rows = wave_table(freq_ids, time_ids, NT, NT ** (-0.5))
    spectra = lax.psum_scatter(
        jnp.einsum("qft,tcx->fqcx", wave_rows, time_slab, precision=HIGHEST_PRECISION),
        "freq",
        scatter_dimension=0,
        tiled=True,
    )
    sketch_basis, gram_raw, cross_raw = lax.map(first_pass, (spectra, probes))
    gram_sum, cross_sum = lax.psum((gram_raw, cross_raw), "space")
    gram_matrix, cross_terms = assemble(gram_sum, cross_sum)
    lower_factor = jnp.linalg.cholesky(gram_matrix)
    coeffs = jax.vmap(solve_one)(lower_factor, cross_terms)
    window = width // 2 + 1
    columns = width // 2

    def second_pass(slice_pair):
        basis_rows, coeff_rows = slice_pair
        half = coeff_rows.shape[0] // 2
        real_part = coeff_rows[:half]
        imag_part = coeff_rows[half:]
        mixing = jnp.stack(
            [
                jnp.concatenate([real_part, -imag_part], 0),
                jnp.concatenate([imag_part, real_part], 0),
            ]
        )
        rebuilt = jnp.einsum("rk,qkp->qrp", basis_rows, mixing, precision=HIGHEST_PRECISION)
        return diag_mean(rebuilt.reshape(2, channels, window, columns), width)

    clean = lax.map(second_pass, (sketch_basis, coeffs))
    start_volume = jnp.zeros((time_local, channels, width), jnp.float32)
    shard_piece = lax.all_gather(clean, "freq", axis=0, tiled=True)
    freq_ids = BAND_LO + jnp.int32(0) + jnp.arange(shard_piece.shape[0], dtype=jnp.int32)
    wave_rows = wave_table(freq_ids, time_ids, NT, (2.0 / freq_total) ** 0.5)
    volume = start_volume + jnp.einsum(
        "qft,fqcx->tcx", wave_rows, shard_piece, precision=HIGHEST_PRECISION
    )
    return lax.all_to_all(volume, "space", split_axis=0, concat_axis=1, tiled=True)


def solution(mesh):
    in_specs = (P(("freq", "space"), None, None), P("freq", None, None))
    out_specs = P(("freq", "space"), None, None)
    return jax.shard_map(body, mesh=mesh, in_specs=in_specs, out_specs=out_specs, check_vma=False)
```

profile of v0, /device:TPU:0, one launch (start us, length us, event | category | flops | bytes accessed | tf_op | source)
XLA Modules:
  0.0 1406.5 jit_solution(224654636673980314)
XLA Ops:
  6.5 17.8 %copy.34 = f32[32,512,256]{2,0,1:T(8,128)} copy(f32[32,512,256]{2,1,0:T(8,128)} %param.6) | data formatting | bytes 33554432 | tf_op args[0]
  32.2 362.5 %all-to-all-done = f32[32,512,256]{2,0,1:T(8,128)} async-done(((f32[32,512,256]{2,0,1:T(8,128)}), f32[32,512,256]{2,0,1:T(8,128)}, u32[]{:S(2)}, u32[]{:S(2)}) %all-to-all-start) | async-done | bytes 16777248 | tf_op jit(solution)/shard_map/all_to_all | solution.py:78
  410.7 23.8 %reduce-scatter.2.cloned.1.call-done = f32[2,2,64,256]{3,2,1,0:T(8,128)} async-done(((f32[8,2,64,256]{3,2,1,0:T(8,128)}), f32[2,2,64,256]{3,2,1,0:T(8,128)}) %reduce-scatter.2.cloned.1.call-update) | async-done | bytes 262160 | tf_op jit(solution)/shard_map/reduce_scatter | solution.py:89
  434.6 237.5 %while.26 = (s32[]{:T(128)}, f32[2,8256,128]{2,1,0:T(8,128)}, f32[2,128,128]{1,2,0:T(8,128)S(1)}, f32[2,2,128,128]{3,2,0,1:T(8,128)S(1)}, f32[2,128,64]{1,2,0:T(...) while((s32[]{:T(128)}, f32[2,8256,128]{2,1,0:T(8,128)}, f32[2,128,128]{1,2,0:T(8,128)S(1)}, ...), condition=%wide.region_2.3_spmd, body=%wide.region_1.2_spmd.sunk | while | flops 6492782592 | bytes 234325712 | solution.py:95
  459.7 18.4 %tile.14 = f32[2,64,33280]{2,1,0:T(8,128)} reshape(f32[2,64,130,256]{3,2,1,0:T(8,128)} %tile.13) | data formatting | bytes 34078720 | tf_op jit(solution)/shard_map/while/body/eval_jaxpr/tile | solution.py:20
  478.1 23.7 %reshape.225 = f32[2,64,129,257]{3,2,1,0:T(8,128)} reshape(f32[2,64,33153]{2,1,0:T(8,128)} %bitcast.128) | data formatting | bytes 33948672 | tf_op jit(solution)/shard_map/while/body/eval_jaxpr/reshape | solution.py:21
  509.7 9.1 reshape.226
  518.8 11.9 fusion.68
  532.8 13.7 convolution_bitcast_fusion.7
  569.9 18.4 %tile.14 = f32[2,64,33280]{2,1,0:T(8,128)} reshape(f32[2,64,130,256]{3,2,1,0:T(8,128)} %tile.13) | data formatting | bytes 34078720 | tf_op jit(solution)/shard_map/while/body/eval_jaxpr/tile | solution.py:20
  588.3 23.7 %reshape.225 = f32[2,64,129,257]{3,2,1,0:T(8,128)} reshape(f32[2,64,33153]{2,1,0:T(8,128)} %bitcast.128) | data formatting | bytes 33948672 | tf_op jit(solution)/shard_map/while/body/eval_jaxpr/reshape | solution.py:21
  619.9 9.1 reshape.226
  629.0 11.9 fusion.68
  643.0 13.7 convolution_bitcast_fusion.7
  672.9 72.1 %all-reduce.5.cloned.1.call-done = (f32[2,2,128,128]{3,2,0,1:T(8,128)}, f32[2,128,128]{1,2,0:T(8,128)}) async-done(((f32[2,2,128,128]{3,2,0,1:T(8,128)}, f32[2,128,128]{1,2,0:T(8,128)}), (f32[2,2,128,128]{3,2,0,1:T(8,128)}, f32[2,128,128]{1,2,0:T(8,128)})) %all-reduce.5.cloned.1.call-update) | async-done | bytes 393232 | tf_op jit(solution)/shard_map/psum | solution.py:96
  746.4 23.5 %custom-call.11 = f32[2,128,128]{2,1,0:T(8,128)S(1)} custom-call(f32[2,128,128]{2,1,0:T(8,128)S(1)} %fusion.24), custom_call_target="Cholesky" | custom-call | tf_op jit(solution)/shard_map/jit(cholesky)/cholesky | solution.py:98
  770.1 19.7 %custom-call.12 = f32[2,1,128,128]{2,3,1,0:T(8,128)S(1)} custom-call(f32[2,1,128,128]{3,2,1,0:T(8,128)S(1)} %select_bitcast_fusion), custom_call_target="InvertDiagBlocksLowerTriangular" | custom-call | tf_op jit(solution)/shard_map/vmap(jit(_cho_solve))/triangular_solve | solution.py:59
  791.5 184.5 %while.27 = (s32[]{:T(128)}, f32[2,2,64,256]{3,2,1,0:T(8,128)S(1)}, f32[2,128,128]{2,1,0:T(8,128)S(1)}, f32[2,8256,128]{2,1,0:T(8,128)}, s32[]{:T(128)}, /*index=5*/s32[]{:T(128)}, s32[]{}, f32[]{:T(128)}) while((s32[]{:T(128)}, f32[2,2,64,256]{3,2,1,0:T(8,128)S(1)}, f32[2,128,128]{2,1,0:T(8,128)S(1)}, f32[2,8256,128]{2,1,0:T(8,128)}, ...), condition=%wide.region_9.10_spmd, body=%wide.region_7.9_spmd.sunk | while | flops 3250726144 | bytes 175018624 | solution.py:117
  791.8 10.5 convolution_bitcast_fusion.8
  811.3 12.3 pad.84
  823.6 22.5 %reshape.228 = f32[2,64,33153]{2,1,0:T(8,128)} reshape(f32[2,64,129,257]{3,2,1,0:T(8,128)} %pad.84) | data formatting | bytes 33948672 | tf_op jit(solution)/shard_map/while/body/eval_jaxpr/reshape | solution.py:27
  846.0 11.4 pad.85
  857.5 18.3 %reshape.229 = f32[2,64,130,256]{3,2,1,0:T(8,128)} reshape(f32[2,64,33280]{2,1,0:T(8,128)} %pad.85) | data formatting | bytes 34078720 | tf_op jit(solution)/shard_map/while/body/eval_jaxpr/reshape | solution.py:29
  884.0 10.5 convolution_bitcast_fusion.8
  903.5 12.3 pad.84
  915.7 22.5 %reshape.228 = f32[2,64,33153]{2,1,0:T(8,128)} reshape(f32[2,64,129,257]{3,2,1,0:T(8,128)} %pad.84) | data formatting | bytes 33948672 | tf_op jit(solution)/shard_map/while/body/eval_jaxpr/reshape | solution.py:27
  938.2 11.4 pad.85
  949.6 18.3 %reshape.229 = f32[2,64,130,256]{3,2,1,0:T(8,128)} reshape(f32[2,64,33280]{2,1,0:T(8,128)} %pad.85) | data formatting | bytes 34078720 | tf_op jit(solution)/shard_map/while/body/eval_jaxpr/reshape | solution.py:29
  976.8 15.9 %all-gather.2.cloned.1.call-done = f32[8,2,64,256]{3,2,1,0:T(8,128)} async-done(((f32[2,2,64,256]{3,2,1,0:T(8,128)}), f32[8,2,64,256]{3,2,1,0:T(8,128)}) %all-gather.2.cloned.1.call-update) | async-done | bytes 1048592 | tf_op jit(solution)/shard_map/all_gather | solution.py:119
  992.7 14.8 %convolution_bitcast_fusion.3 = f32[256,64,256]{2,0,1:T(8,128)S(1)} fusion(f32[8,2,64,256]{3,2,1,0:T(8,128)} %all-gather.2.cloned.1.call-done, f32[1,8,256]{2,1,0:T(8,128)S(1)} %copy-done.9, f32[1,8,256]{2,1,0:T(8,128)S(1)} %copy-done.7), kind=kOutput, calls=%fused_computation.29 | convolution fusion | flops 805314560 | bytes 17842176 | tf_op jit(solution)/shard_map/qft,fqcx->tcx/dot_general | solution.py:122
  1007.5 17.6 %copy.43 = f32[256,64,256]{2,1,0:T(8,128)S(1)} copy(f32[256,64,256]{2,0,1:T(8,128)S(1)} %convolution_bitcast_fusion.3) | data formatting | bytes 33554432 | tf_op jit(solution)/shard_map/qft,fqcx->tcx/dot_general | solution.py:122
  1025.1 368.5 %all_to_all.36 = f32[256,64,256]{2,1,0:T(8,128)S(1)} all-to-all(f32[256,64,256]{2,1,0:T(8,128)S(1)} %copy.43), channel_id=1, replica_groups=mesh['freq'=4,'space'=8] {'space'}, dimensions={0} | all-to-all | bytes 33554432 | tf_op jit(solution)/shard_map/all_to_all | solution.py:125
  (95 shorter events, 135.9 us)
Async XLA Ops:
  24.3 370.4 %all-to-all-start = ((f32[32,512,256]{2,0,1:T(8,128)}), f32[32,512,256]{2,0,1:T(8,128)}, u32[]{:S(2)}, u32[]{:S(2)}) async-start(f32[32,512,256]{2,0,1:T(8,128)} %copy.34), calls=%async_computation | async-start | bytes 33554432 | tf_op jit(solution)/shard_map/all_to_all | solution.py:78
  31.6 403.0 %reduce-scatter.2.cloned.1.call-start = ((), (), s32[]{:S(2)}) async-start(), calls=%async_computation.3 | async-start | bytes 1310720 | tf_op jit(solution)/shard_map/reduce_scatter | solution.py:89
  32.2 369.1 %copy-start.6 = (f32[1,8,256]{2,1,0:T(8,128)}, f32[1,8,256]{2,1,0:T(8,128)S(1)}, u32[]{:S(2)}) copy-start(f32[1,8,256]{2,1,0:T(8,128)S(1)} %get-tuple-element.157) | copy-start | bytes 24580
  32.2 369.1 %copy-start.8 = (f32[1,8,256]{2,1,0:T(8,128)}, f32[1,8,256]{2,1,0:T(8,128)S(1)}, u32[]{:S(2)}) copy-start(f32[1,8,256]{2,1,0:T(8,128)S(1)} %get-tuple-element.158) | copy-start | bytes 24580
  401.3 33.2 %copy-start.2 = (f32[2,128,64]{1,2,0:T(8,128)S(1)}, f32[2,128,64]{1,2,0:T(8,128)}, u32[]{:S(2)}) copy-start(f32[2,128,64]{1,2,0:T(8,128)} %param.7) | copy-start | bytes 196612
  410.6 334.4 %all-reduce.5.cloned.1.call-start = ((), (), s32[]{:S(2)}) async-start(), calls=%async_computation.5 | async-start | bytes 786432 | tf_op jit(solution)/shard_map/psum | solution.py:96
  518.8 14.0 copy-start.1
  530.7 2.0 copy-start
  552.3 5.0 slice-start
  552.3 5.0 slice-start.1
  629.0 14.0 copy-start.1
  640.9 2.0 copy-start
  662.5 5.0 slice-start
  662.5 5.0 slice-start.1
  672.1 0.7 copy-start.3
  672.1 0.7 copy-start.5
  672.8 319.8 %all-gather.2.cloned.1.call-start = ((), (), s32[]{:S(2)}) async-start(), calls=%async_computation.4 | async-start | bytes 1310720 | tf_op jit(solution)/shard_map/all_gather | solution.py:119
  791.5 201.1 %copy-start.7 = (f32[1,8,256]{2,1,0:T(8,128)S(1)}, f32[1,8,256]{2,1,0:T(8,128)}, u32[]{:S(2)}) copy-start(f32[1,8,256]{2,1,0:T(8,128)} %copy-done.6) | copy-start | bytes 24580
  791.5 201.1 %copy-start.9 = (f32[1,8,256]{2,1,0:T(8,128)S(1)}, f32[1,8,256]{2,1,0:T(8,128)}, u32[]{:S(2)}) copy-start(f32[1,8,256]{2,1,0:T(8,128)} %copy-done.8) | copy-start | bytes 24580
  976.1 0.7 copy-start.4
Sparse Core Ops, SparseCore 0:
  410.8 23.7 reduce-scatter.1
  673.0 72.0 all-reduce.4
  976.9 15.7 all-gather.1
where the time goes:
time: 1420 us; the launch traced here: 1410 us
  waiting for transfers between devices  474 us (33%)
  blocking collectives  368 us (26%)
  local copies, waits for them, and re-layouts  360 us (25%)
  matrix products  104 us (7%)
  other arithmetic  61 us (4%)
  loops' own time  17.5 us (1%)
    all_to_all x1, blocking collectives, body(): lax.all_to_all(volume, 'space', split_axis=0, concat_axis=1, tiled=True)  368 us
    all_to_all x1, waiting for transfers between devices, body(): lax.all_to_all(traces, 'space', split_axis=1, concat_axis=0, tiled=True)  362 us
    psum x1, waiting for transfers between devices, body(): gram_sum, cross_sum = lax.psum((gram_raw, cross_raw), 'space')  72.1 us
    another operation x6, local copies, waits for them, and re-layouts, hankel(): tiled = jnp.tile(spectrum, (1, 1, window + 1))[:, :, :window * (width + 1)]  53.7 us
    reshape x2, local copies, waits for them, and re-layouts, hankel(): tiled.reshape(spectrum.shape[0], spectrum.shape[1], window, width + 1)  47.4 us
    reshape x2, local copies, waits for them, and re-layouts, diag_mean(): flat_rows = padded.reshape(halves, channels, window * (width + 1))  44.9 us
    reshape x2, local copies, waits for them, and re-layouts, diag_mean(): totals = flat_rows.reshape(halves, channels, window + 1, width).sum(axis=2)  36.6 us
  transfers between devices with their start and end apart: 4, of which 4 were waited for; matrix products, arithmetic and copies ran while one was open for 0% of the time, Pallas kernels for 0%

commit v1 on v0

--- a/solution.py
+++ b/solution.py
@@ -6,6 +6,13 @@
 NT = 1024
 BAND_LO = 16
 HIGHEST_PRECISION = lax.Precision.HIGHEST
+
+
+def stacked_exchange(x, axis, split, join):
+    size = lax.axis_size(axis)
+    parts = jnp.stack(jnp.split(x, size, axis=split), axis=0)
+    parts = lax.all_to_all(parts, axis, split_axis=0, concat_axis=0)
+    return jnp.concatenate(parts, axis=join)
 
 
 def wave_table(freq_ids, time_ids, period, factor):
@@ -122,7 +129,7 @@
     volume = start_volume + jnp.einsum(
         "qft,fqcx->tcx", wave_rows, shard_piece, precision=HIGHEST_PRECISION
     )
-    return lax.all_to_all(volume, "space", split_axis=0, concat_axis=1, tiled=True)
+    return stacked_exchange(volume, "space", 0, 1)
 
 
 def solution(mesh):

time: 1420 us -> 1420 us (level)
    reshape x0 -> x1, local copies, waits for them, and re-layouts: none -> 19.3 us  [stacked_exchange(): return jnp.concatenate(parts, axis=join)]
    dot_general x1 -> x0, local copies, waits for them, and re-layouts: 17.6 us -> none  [body(): jnp.einsum('qft,fqcx->tcx', wave_rows, shard_piece, precision=HIGHEST_PRE...]
where the time goes in v1:
time: 1420 us; the launch traced here: 1410 us
  waiting for transfers between devices  474 us (33%)
  blocking collectives  369 us (26%)
  local copies, waits for them, and re-layouts  353 us (25%)
  matrix products  111 us (8%)
  other arithmetic  61 us (4%)
  loops' own time  17.5 us (1%)
    all_to_all x1, blocking collectives, stacked_exchange(): parts = lax.all_to_all(parts, axis, split_axis=0, concat_axis=0)  369 us
    all_to_all x1, waiting for transfers between devices, body(): lax.all_to_all(traces, 'space', split_axis=1, concat_axis=0, tiled=True)  362 us
    psum x1, waiting for transfers between devices, body(): gram_sum, cross_sum = lax.psum((gram_raw, cross_raw), 'space')  72.1 us
    another operation x6, local copies, waits for them, and re-layouts, hankel(): tiled = jnp.tile(spectrum, (1, 1, window + 1))[:, :, :window * (width + 1)]  53.7 us
    reshape x2, local copies, waits for them, and re-layouts, hankel(): tiled.reshape(spectrum.shape[0], spectrum.shape[1], window, width + 1)  47.3 us
    reshape x2, local copies, waits for them, and re-layouts, diag_mean(): flat_rows = padded.reshape(halves, channels, window * (width + 1))  44.9 us
    reshape x2, local copies, waits for them, and re-layouts, diag_mean(): totals = flat_rows.reshape(halves, channels, window + 1, width).sum(axis=2)  36.6 us
  transfers between devices with their start and end apart: 4, of which 4 were waited for; matrix products, arithmetic and copies ran while one was open for 0% of the time, Pallas kernels for 0%

profile of v1, /device:TPU:0, one launch (start us, length us, event | category | flops | bytes accessed | tf_op | source)
XLA Modules:
  0.0 1407.6 jit_solution(4780748302705515981)
XLA Ops:
  6.5 17.8 %copy.33 = f32[32,512,256]{2,0,1:T(8,128)} copy(f32[32,512,256]{2,1,0:T(8,128)} %param.6) | data formatting | bytes 33554432 | tf_op args[0]
  32.3 362.4 %all-to-all-done = f32[32,512,256]{2,0,1:T(8,128)} async-done(((f32[32,512,256]{2,0,1:T(8,128)}), f32[32,512,256]{2,0,1:T(8,128)}, u32[]{:S(2)}, u32[]{:S(2)}) %all-to-all-start) | async-done | bytes 16777248 | tf_op jit(solution)/shard_map/all_to_all | solution.py:85
  410.7 23.9 %reduce-scatter.2.cloned.1.call-done = f32[2,2,64,256]{3,2,1,0:T(8,128)} async-done(((f32[8,2,64,256]{3,2,1,0:T(8,128)}), f32[2,2,64,256]{3,2,1,0:T(8,128)}) %reduce-scatter.2.cloned.1.call-update) | async-done | bytes 262160 | tf_op jit(solution)/shard_map/reduce_scatter | solution.py:96
  434.6 241.6 %while.26 = (s32[]{:T(128)}, f32[2,8256,128]{2,1,0:T(8,128)}, f32[2,128,128]{1,2,0:T(8,128)S(1)}, f32[2,2,128,128]{3,2,0,1:T(8,128)S(1)}, f32[2,128,64]{1,2,0:T(...) while((s32[]{:T(128)}, f32[2,8256,128]{2,1,0:T(8,128)}, f32[2,128,128]{1,2,0:T(8,128)S(1)}, ...), condition=%wide.region_2.3_spmd, body=%wide.region_1.2_spmd.sunk | while | flops 6492782592 | bytes 221546640 | solution.py:102
  459.8 18.4 %tile.14 = f32[2,64,33280]{2,1,0:T(8,128)} reshape(f32[2,64,130,256]{3,2,1,0:T(8,128)} %tile.13) | data formatting | bytes 34078720 | tf_op jit(solution)/shard_map/while/body/eval_jaxpr/tile | solution.py:27
  478.1 23.6 %reshape.233 = f32[2,64,129,257]{3,2,1,0:T(8,128)} reshape(f32[2,64,33153]{2,1,0:T(8,128)} %bitcast.157) | data formatting | bytes 33948672 | tf_op jit(solution)/shard_map/while/body/eval_jaxpr/reshape | solution.py:28
  509.6 9.1 reshape.234
  518.6 11.9 fusion.76
  532.6 13.7 convolution_bitcast_fusion.7
  572.0 18.4 %tile.14 = f32[2,64,33280]{2,1,0:T(8,128)} reshape(f32[2,64,130,256]{3,2,1,0:T(8,128)} %tile.13) | data formatting | bytes 34078720 | tf_op jit(solution)/shard_map/while/body/eval_jaxpr/tile | solution.py:27
  590.4 23.6 %reshape.233 = f32[2,64,129,257]{3,2,1,0:T(8,128)} reshape(f32[2,64,33153]{2,1,0:T(8,128)} %bitcast.157) | data formatting | bytes 33948672 | tf_op jit(solution)/shard_map/while/body/eval_jaxpr/reshape | solution.py:28
  621.8 9.1 reshape.234
  630.9 11.9 fusion.76
  644.8 13.7 convolution_bitcast_fusion.7
  677.1 72.1 %all-reduce.5.cloned.1.call-done = (f32[2,2,128,128]{3,2,0,1:T(8,128)}, f32[2,128,128]{1,2,0:T(8,128)}) async-done(((f32[2,2,128,128]{3,2,0,1:T(8,128)}, f32[2,128,128]{1,2,0:T(8,128)}), (f32[2,2,128,128]{3,2,0,1:T(8,128)}, f32[2,128,128]{1,2,0:T(8,128)})) %all-reduce.5.cloned.1.call-update) | async-done | bytes 393232 | tf_op jit(solution)/shard_map/psum | solution.py:103
  750.6 23.5 %custom-call.11 = f32[2,128,128]{2,1,0:T(8,128)S(1)} custom-call(f32[2,128,128]{2,1,0:T(8,128)S(1)} %fusion.32), custom_call_target="Cholesky" | custom-call | tf_op jit(solution)/shard_map/jit(cholesky)/cholesky | solution.py:105
  774.3 19.7 %custom-call.12 = f32[2,1,128,128]{2,3,1,0:T(8,128)S(1)} custom-call(f32[2,1,128,128]{3,2,1,0:T(8,128)S(1)} %select_bitcast_fusion), custom_call_target="InvertDiagBlocksLowerTriangular" | custom-call | tf_op jit(solution)/shard_map/vmap(jit(_cho_solve))/triangular_solve | solution.py:66
  795.7 184.5 %while.27 = (s32[]{:T(128)}, f32[2,2,64,256]{3,2,1,0:T(8,128)S(1)}, f32[2,128,128]{2,1,0:T(8,128)S(1)}, f32[2,8256,128]{2,1,0:T(8,128)}, s32[]{:T(128)}, /*index=5*/s32[]{:T(128)}, s32[]{}, f32[]{:T(128)}) while((s32[]{:T(128)}, f32[2,2,64,256]{3,2,1,0:T(8,128)S(1)}, f32[2,128,128]{2,1,0:T(8,128)S(1)}, f32[2,8256,128]{2,1,0:T(8,128)}, ...), condition=%wide.region_9.10_spmd, body=%wide.region_7.9_spmd.sunk | while | flops 3250726144 | bytes 175018624 | solution.py:124
  795.9 10.5 convolution_bitcast_fusion.8
  815.4 12.3 pad.84
  827.7 22.5 %reshape.236 = f32[2,64,33153]{2,1,0:T(8,128)} reshape(f32[2,64,129,257]{3,2,1,0:T(8,128)} %pad.84) | data formatting | bytes 33948672 | tf_op jit(solution)/shard_map/while/body/eval_jaxpr/reshape | solution.py:34
  850.2 11.4 pad.85
  861.6 18.3 %reshape.237 = f32[2,64,130,256]{3,2,1,0:T(8,128)} reshape(f32[2,64,33280]{2,1,0:T(8,128)} %pad.85) | data formatting | bytes 34078720 | tf_op jit(solution)/shard_map/while/body/eval_jaxpr/reshape | solution.py:36
  888.1 10.5 convolution_bitcast_fusion.8
  907.6 12.3 pad.84
  919.9 22.5 %reshape.236 = f32[2,64,33153]{2,1,0:T(8,128)} reshape(f32[2,64,129,257]{3,2,1,0:T(8,128)} %pad.84) | data formatting | bytes 33948672 | tf_op jit(solution)/shard_map/while/body/eval_jaxpr/reshape | solution.py:34
  942.3 11.4 pad.85
  953.8 18.3 %reshape.237 = f32[2,64,130,256]{3,2,1,0:T(8,128)} reshape(f32[2,64,33280]{2,1,0:T(8,128)} %pad.85) | data formatting | bytes 34078720 | tf_op jit(solution)/shard_map/while/body/eval_jaxpr/reshape | solution.py:36
  980.9 15.9 %all-gather.2.cloned.1.call-done = f32[8,2,64,256]{3,2,1,0:T(8,128)} async-done(((f32[2,2,64,256]{3,2,1,0:T(8,128)}), f32[8,2,64,256]{3,2,1,0:T(8,128)}) %all-gather.2.cloned.1.call-update) | async-done | bytes 1048592 | tf_op jit(solution)/shard_map/all_gather | solution.py:126
  996.8 14.8 %convolution_bitcast_fusion.3 = f32[256,64,256]{2,0,1:T(8,128)S(1)} fusion(f32[8,2,64,256]{3,2,1,0:T(8,128)} %all-gather.2.cloned.1.call-done, f32[1,8,256]{2,1,0:T(8,128)S(1)} %copy-done.9, f32[1,8,256]{2,1,0:T(8,128)S(1)} %copy-done.7), kind=kOutput, calls=%fused_computation.29 | convolution fusion | flops 805314560 | bytes 17842176 | tf_op jit(solution)/shard_map/qft,fqcx->tcx/dot_general | solution.py:129
  1012.8 368.7 %all_to_all.23 = f32[8,32,64,256]{3,1,2,0:T(8,128)S(1)} all-to-all(f32[8,32,64,256]{3,1,2,0:T(8,128)S(1)} %fusion.16), channel_id=1, replica_groups=mesh['freq'=4,'space'=8] {'space'}, dimensions={0} | all-to-all | bytes 33554432 | tf_op jit(solution)/shard_map/all_to_all | solution.py:14
  1381.5 19.3 %copy.42 = f32[32,512,256]{2,1,0:T(8,128)} copy(f32[32,512,256]{2,0,1:T(8,128)S(1)} %bitcast.159) | data formatting | bytes 33554432 | tf_op jit(solution)/shard_map/reshape | solution.py:15
  (92 shorter events, 135.0 us)
Async XLA Ops:
  24.3 370.4 %all-to-all-start = ((f32[32,512,256]{2,0,1:T(8,128)}), f32[32,512,256]{2,0,1:T(8,128)}, u32[]{:S(2)}, u32[]{:S(2)}) async-start(f32[32,512,256]{2,0,1:T(8,128)} %copy.33), calls=%async_computation | async-start | bytes 33554432 | tf_op jit(solution)/shard_map/all_to_all | solution.py:85
  31.6 403.0 %reduce-scatter.2.cloned.1.call-start = ((), (), s32[]{:S(2)}) async-start(), calls=%async_computation.3 | async-start | bytes 1310720 | tf_op jit(solution)/shard_map/reduce_scatter | solution.py:96
  32.3 369.0 %copy-start.6 = (f32[1,8,256]{2,1,0:T(8,128)}, f32[1,8,256]{2,1,0:T(8,128)S(1)}, u32[]{:S(2)}) copy-start(f32[1,8,256]{2,1,0:T(8,128)S(1)} %get-tuple-element.157) | copy-start | bytes 24580
  32.3 369.0 %copy-start.8 = (f32[1,8,256]{2,1,0:T(8,128)}, f32[1,8,256]{2,1,0:T(8,128)S(1)}, u32[]{:S(2)}) copy-start(f32[1,8,256]{2,1,0:T(8,128)S(1)} %get-tuple-element.158) | copy-start | bytes 24580
  401.3 33.3 %copy-start.2 = (f32[2,128,64]{1,2,0:T(8,128)S(1)}, f32[2,128,64]{1,2,0:T(8,128)}, u32[]{:S(2)}) copy-start(f32[2,128,64]{1,2,0:T(8,128)} %param.7) | copy-start | bytes 196612
  410.6 338.6 %all-reduce.5.cloned.1.call-start = ((), (), s32[]{:S(2)}) async-start(), calls=%async_computation.5 | async-start | bytes 786432 | tf_op jit(solution)/shard_map/psum | solution.py:103
  518.6 14.0 copy-start.1
  530.6 2.0 copy-start
  630.9 14.0 copy-start.1
  642.8 2.0 copy-start
  676.2 0.7 copy-start.3
  676.2 0.7 copy-start.5
  677.0 319.8 %all-gather.2.cloned.1.call-start = ((), (), s32[]{:S(2)}) async-start(), calls=%async_computation.4 | async-start | bytes 1310720 | tf_op jit(solution)/shard_map/all_gather | solution.py:126
  795.6 201.2 %copy-start.7 = (f32[1,8,256]{2,1,0:T(8,128)S(1)}, f32[1,8,256]{2,1,0:T(8,128)}, u32[]{:S(2)}) copy-start(f32[1,8,256]{2,1,0:T(8,128)} %copy-done.6) | copy-start | bytes 24580
  795.7 201.2 %copy-start.9 = (f32[1,8,256]{2,1,0:T(8,128)S(1)}, f32[1,8,256]{2,1,0:T(8,128)}, u32[]{:S(2)}) copy-start(f32[1,8,256]{2,1,0:T(8,128)} %copy-done.8) | copy-start | bytes 24580
  980.2 0.7 copy-start.4
Sparse Core Ops, SparseCore 0:
  410.8 23.7 reduce-scatter.1
  677.1 72.0 all-reduce.4
  981.0 15.7 all-gather.1
